TPU v7x, 32 devices: a whole 2x2x4 slice. The times are simulated.
32 devices in a mesh: rows: 8 (over z, y), cols: 4 (over x, core).
Axes of the slice: x: 2, y: 2, z: 4, core: 2. Of those that a mesh axis runs over, the one named last changes fastest.
Arguments:
- sketches: bfloat16 [2048, 16384], P('rows', 'cols'), may hold values from -6 to 6, as said below
- start_basis: bfloat16 [16384, 256], P('cols'), may hold values from -6 to 6
- shrink_index: int32 [1], replicated, may hold values from 64 to 191
Outputs:
- shrunk: float32 [256, 16384], P('rows', 'cols')
Inputs may be any that keep to these rules, and one draw needn't show every extreme that they name: `sketches`: real entries.
All inputs are finite; a program needn't handle non-finite values.
Results may differ from a plain program's by a relative error of at most 0.0028.
Values may be sent and summed in bfloat16 or wider, within the bound.
A program may use at most 64 MiB of HBM per device.

v0:
```python
import jax
import jax.numpy as jnp
from jax import lax
from jax.sharding import PartitionSpec as P

ITERS = 3
AXES = ("rows", "cols")
HIGHEST = lax.Precision.HIGHEST


def pieces(values):
    high = lax.reduce_precision(values, 8, 7)
    rest = values - high
    middle = lax.reduce_precision(rest, 8, 7)
    low = rest - middle
    return [part.astype(jnp.bfloat16) for part in (high, middle, low)]


def apply_sketches(strip, images):
    stacked = jnp.concatenate(pieces(images), axis=1)
    products = jnp.dot(strip, stacked, preferred_element_type=jnp.float32)
    high, middle, low = jnp.split(products, 3, axis=1)
    return high + (middle + low)


def all_sum(values):
    return lax.psum(values, AXES)


def inverse_factor(gram_total):
    lower_factor = jnp.linalg.cholesky(gram_total)
    identity = jnp.eye(gram_total.shape[0], dtype=jnp.float32)
    return jax.scipy.linalg.solve_triangular(lower_factor, identity, lower=True)


def body(sketches, start_basis, shrink_index):
    size = lax.axis_size("rows")
    strip = lax.all_to_all(sketches, "rows", split_axis=1, concat_axis=0, tiled=True)
    width = start_basis.shape[0] // size
    own_basis = lax.dynamic_slice_in_dim(start_basis, lax.axis_index("rows") * width, width, 0)
    projected = all_sum(jnp.dot(strip, own_basis, preferred_element_type=jnp.float32))
    for loop_index in range(ITERS):
        projected_bf = projected.astype(jnp.bfloat16)
        images = jnp.einsum("lw,lk->wk", strip, projected_bf, preferred_element_type=jnp.float32)
        raw = all_sum(apply_sketches(strip, images))
        gram_total = jnp.dot(projected_bf.astype(jnp.float32).T, raw, precision=HIGHEST)
        gram_total = 0.5 * (gram_total + gram_total.T)
        inverse = inverse_factor(gram_total)
        projected = jnp.dot(raw, inverse.T, precision=HIGHEST)
    energy = jnp.sum(projected * projected, axis=0)
    ordered = jnp.sort(energy)[::-1]
    threshold = lax.dynamic_index_in_dim(ordered, shrink_index[0], 0, keepdims=False)
    factor = jnp.sqrt(jnp.maximum(energy - threshold, 0.25 * threshold))
    scaled = jnp.dot(inverse * factor[:, None], images.T, precision=HIGHEST)
    return lax.all_to_all(scaled, "rows", split_axis=0, concat_axis=1, tiled=True)


def solution(mesh):
    return jax.shard_map(
        body,
        mesh=mesh,
        in_specs=(P("rows", "cols"), P("cols", None), P()),
        out_specs=P("rows", "cols"),
        check_vma=False,
    )
```

profile of v0, /device:TPU:0, one launch (start us, length us, event | category | flops | bytes accessed | tf_op | source)
XLA Modules:
  0.0 797.4 jit_solution(12065096326215861704)
XLA Ops:
  6.5 4.3 copy.18
  10.8 7.3 all-to-all-start
  18.1 48.3 %all-to-all-done = bf16[256,8,512]{0,2,1:T(8,128)(2,1)} async-done(((bf16[256,8,512]{0,2,1:T(8,128)(2,1)}), bf16[256,8,512]{0,2,1:T(8,128)(2,1)}, u32[]{:S(2)}, u32[]{:S(2)}) %all-to-all-start) | async-done | bytes 2097184 | tf_op jit(solution)/shard_map/all_to_all | solution.py:38
  66.4 3.9 copy.19
  70.4 3.6 convolution_bitcast_fusion.3
  74.0 59.7 %all-reduce.11 = bf16[2048,256]{0,1:T(8,128)(2,1)S(1)} all-reduce(f32[2048,256]{0,1:T(8,128)} %convolution_bitcast_fusion.3), channel_id=1, replica_groups=mesh['rows'=8,'cols'=4] {'rows','cols'}, use_global_device_ids=true, to_apply=%region_0.0 | all-reduce | flops 524288 | bytes 3145728 | tf_op jit(solution)/shard_map/psum | solution.py:27
  133.8 2.5 reduce-precision_convert_fusion.5
  136.3 1.8 convolution_bitcast_fusion.2
  138.1 1.8 fusion.2
  140.4 133.4 %all-reduce.6.cloned.1.call-done = f32[2048,256]{0,1:T(8,128)} async-done(((f32[2048,256]{0,1:T(8,128)}), f32[2048,256]{0,1:T(8,128)}) %all-reduce.6.cloned.1.call-update) | async-done | bytes 2097168 | tf_op jit(solution)/shard_map/psum | solution.py:27
  273.7 3.5 fusion.84
  277.2 1.1 copy.20
  278.3 1.0 fusion.36
  279.5 11.7 %cholesky.172 = f32[128,128]{1,0:T(8,128)S(1)} custom-call(f32[128,128]{1,0:T(8,128)S(1)} %cholesky.270), custom_call_target="Cholesky" | custom-call | tf_op jit(solution)/shard_map/jit(cholesky)/cholesky | solution.py:31
  291.2 9.8 %custom-call.15 = f32[1,128,128]{1,2,0:T(8,128)S(1)} custom-call(f32[1,128,128]{2,1,0:T(8,128)S(1)} %get-tuple-element.83), custom_call_target="InvertDiagBlocksLowerTriangular" | custom-call | tf_op jit(solution)/shard_map/jit(cholesky)/cholesky | solution.py:31
  301.5 11.7 %cholesky.189 = f32[128,128]{1,0:T(8,128)S(1)} custom-call(f32[128,128]{1,0:T(8,128)S(1)} %convolution_subtract_fusion.5), custom_call_target="Cholesky" | custom-call | tf_op jit(solution)/shard_map/jit(cholesky)/cholesky | solution.py:31
  313.3 0.7 compare_reduce_fusion.4
  315.3 4.5 while.6
  316.5 1.4 bitcast_dynamic-update-slice_fusion.6
  318.4 1.4 bitcast_dynamic-update-slice_fusion.6
  319.8 19.7 %custom-call.16 = f32[2,128,128]{1,2,0:T(8,128)S(1)} custom-call(f32[2,128,128]{2,1,0:T(8,128)S(1)} %get-tuple-element.30), custom_call_target="InvertDiagBlocksLowerTriangular" | custom-call | tf_op jit(solution)/shard_map/jit(_solve_triangular)/triangular_solve | solution.py:33
  340.4 5.1 convolution_convert_fusion.1
  345.5 0.8 reduce-precision_convert_fusion.3
  346.3 1.8 convolution_bitcast_fusion.1
  348.1 1.8 fusion.1
  350.2 133.4 %all-reduce.8.cloned.1.call-done = f32[2048,256]{0,1:T(8,128)} async-done(((f32[2048,256]{0,1:T(8,128)}), f32[2048,256]{0,1:T(8,128)}) %all-reduce.8.cloned.1.call-update) | async-done | bytes 2097168 | tf_op jit(solution)/shard_map/psum | solution.py:27
  483.5 3.7 fusion.82
  487.3 1.1 copy.22
  488.4 1.0 fusion.34
  489.5 11.7 %cholesky.206 = f32[128,128]{1,0:T(8,128)S(1)} custom-call(f32[128,128]{1,0:T(8,128)S(1)} %cholesky.273), custom_call_target="Cholesky" | custom-call | tf_op jit(solution)/shard_map/jit(cholesky)/cholesky | solution.py:31
  501.3 9.8 %custom-call.17 = f32[1,128,128]{1,2,0:T(8,128)S(1)} custom-call(f32[1,128,128]{2,1,0:T(8,128)S(1)} %get-tuple-element.79), custom_call_target="InvertDiagBlocksLowerTriangular" | custom-call | tf_op jit(solution)/shard_map/jit(cholesky)/cholesky | solution.py:31
  511.6 11.7 %cholesky.223 = f32[128,128]{1,0:T(8,128)S(1)} custom-call(f32[128,128]{1,0:T(8,128)S(1)} %convolution_subtract_fusion.4), custom_call_target="Cholesky" | custom-call | tf_op jit(solution)/shard_map/jit(cholesky)/cholesky | solution.py:31
  523.4 0.6 compare_reduce_fusion.2
  524.0 0.6 compare_reduce_fusion.3
  526.0 3.9 while.7
  526.6 1.4 bitcast_dynamic-update-slice_fusion.7
  528.5 1.4 bitcast_dynamic-update-slice_fusion.7
  529.9 19.9 %custom-call.18 = f32[2,128,128]{1,2,0:T(8,128)S(1)} custom-call(f32[2,128,128]{2,1,0:T(8,128)S(1)} %get-tuple-element.31), custom_call_target="InvertDiagBlocksLowerTriangular" | custom-call | tf_op jit(solution)/shard_map/jit(_solve_triangular)/triangular_solve | solution.py:33
  550.7 5.1 convolution_convert_fusion
  555.8 1.5 reduce-precision_convert_fusion.1
  557.3 1.8 convolution_bitcast_fusion
  559.2 1.8 fusion
  561.7 132.9 %all-reduce.10.cloned.1.call-done = f32[2048,256]{0,1:T(8,128)} async-done(((f32[2048,256]{0,1:T(8,128)}), f32[2048,256]{0,1:T(8,128)}) %all-reduce.10.cloned.1.call-update) | async-done | bytes 2097168 | tf_op jit(solution)/shard_map/psum | solution.py:27
  694.5 3.8 fusion.83
  698.3 1.1 copy.24
  699.4 1.0 fusion.32
  700.6 11.7 %cholesky.240 = f32[128,128]{1,0:T(8,128)S(1)} custom-call(f32[128,128]{1,0:T(8,128)S(1)} %cholesky.276), custom_call_target="Cholesky" | custom-call | tf_op jit(solution)/shard_map/jit(cholesky)/cholesky | solution.py:31
  712.3 10.2 %custom-call.19 = f32[1,128,128]{1,2,0:T(8,128)S(1)} custom-call(f32[1,128,128]{2,1,0:T(8,128)S(1)} %get-tuple-element.75), custom_call_target="InvertDiagBlocksLowerTriangular" | custom-call | tf_op jit(solution)/shard_map/jit(cholesky)/cholesky | solution.py:31
  723.0 11.7 %cholesky.257 = f32[128,128]{1,0:T(8,128)S(1)} custom-call(f32[128,128]{1,0:T(8,128)S(1)} %convolution_subtract_fusion.3), custom_call_target="Cholesky" | custom-call | tf_op jit(solution)/shard_map/jit(cholesky)/cholesky | solution.py:31
  734.8 0.7 compare_reduce_fusion
  735.4 0.6 compare_reduce_fusion.1
  737.4 3.9 while.8
  737.4 0.6 fusion.122
  738.0 1.3 bitcast_dynamic-update-slice_fusion.8
  739.3 0.6 fusion.122
  739.9 1.3 bitcast_dynamic-update-slice_fusion.8
  741.3 19.8 %custom-call.20 = f32[2,128,128]{1,2,0:T(8,128)S(1)} custom-call(f32[2,128,128]{2,1,0:T(8,128)S(1)} %get-tuple-element.32), custom_call_target="InvertDiagBlocksLowerTriangular" | custom-call | tf_op jit(solution)/shard_map/jit(_solve_triangular)/triangular_solve | solution.py:33
  762.0 5.0 fusion.3
  767.1 3.3 sort.15
  770.5 0.7 dynamic_slice.8
  771.8 0.7 maximum_sqrt_fusion
  772.5 0.6 fusion.37
  773.2 16.7 %all_to_all.38 = f32[8,32,512]{2,1,0:T(8,128)S(1)} all-to-all(f32[8,32,512]{2,1,0:T(8,128)S(1)} %bitcast.164), channel_id=1, replica_groups=mesh['rows'=8,'cols'=4] {'rows'}, dimensions={0} | all-to-all | bytes 1048576 | tf_op jit(solution)/shard_map/all_to_all | solution.py:55
  789.8 0.8 copy.27
  (70 shorter events, 8.2 us)
Async XLA Ops:
  6.5 63.8 %copy-start = (bf16[4096,256]{1,0:T(8,128)(2,1)S(1)}, bf16[4096,256]{1,0:T(8,128)(2,1)}, u32[]{:S(2)}) copy-start(bf16[4096,256]{1,0:T(8,128)(2,1)} %param.7) | copy-start | bytes 6291460
  10.8 55.7 %all-to-all-start = ((bf16[256,8,512]{0,2,1:T(8,128)(2,1)}), bf16[256,8,512]{0,2,1:T(8,128)(2,1)}, u32[]{:S(2)}, u32[]{:S(2)}) async-start(bf16[256,8,512]{0,2,1:T(8,128)(2,1)} %bitcast.163), calls=%async_computation | async-start | bytes 4194304 | tf_op jit(solution)/shard_map/all_to_all | solution.py:38
  18.1 255.6 %all-reduce.6.cloned.1.call-start = ((), (), s32[]{:S(2)}) async-start(), calls=%async_computation.2 | async-start | bytes 4194304 | tf_op jit(solution)/shard_map/psum | solution.py:27
  133.8 2.5 copy-start.1
  140.0 343.6 %all-reduce.8.cloned.1.call-start = ((), (), s32[]{:S(2)}) async-start(), calls=%async_computation.3 | async-start | bytes 4194304 | tf_op jit(solution)/shard_map/psum | solution.py:27
  339.8 5.7 copy-start.2
  350.0 344.6 %all-reduce.10.cloned.1.call-start = ((), (), s32[]{:S(2)}) async-start(), calls=%async_computation.4 | async-start | bytes 4194304 | tf_op jit(solution)/shard_map/psum | solution.py:27
  550.1 5.7 copy-start.3
  737.4 35.2 %copy-start.4 = (f32[256,512]{1,0:T(8,128)S(1)}, f32[256,512]{1,0:T(8,128)}, u32[]{:S(2)}) copy-start(f32[256,512]{1,0:T(8,128)} %get-tuple-element.88) | copy-start | bytes 1572868
Sparse Core Ops, SparseCore 0:
  140.1 133.5 all-reduce.5
  350.1 133.4 all-reduce.7
  561.1 133.3 all-reduce.9
where the time goes:
time: 802 us; the launch traced here: 797 us
  waiting for transfers between devices  448 us (56%)
  other arithmetic  176 us (22%)
  blocking collectives  76.4 us (10%)
  matrix products  44.7 us (6%)
  local copies, waits for them, and re-layouts  25.2 us (3%)
  between operations  18.9 us (2%)
    psum x3, waiting for transfers between devices, all_sum(): return lax.psum(values, AXES)  400 us
    another operation x20, other arithmetic, inverse_factor(): lower_factor = jnp.linalg.cholesky(gram_total)  104 us
    psum x1, blocking collectives, all_sum(): return lax.psum(values, AXES)  59.7 us
    another operation x7, other arithmetic, inverse_factor(): return jax.scipy.linalg.solve_triangular(lower_factor, identity, lower=True)  59.5 us
    all_to_all x1, waiting for transfers between devices, body(): lax.all_to_all(sketches, 'rows', split_axis=1, concat_axis=0, tiled=True)  48.3 us
    all_to_all x1, blocking collectives, body(): lax.all_to_all(scaled, 'rows', split_axis=0, concat_axis=1, tiled=True)  16.7 us
  transfers between devices with their start and end apart: 4, of which 4 were waited for; matrix products, arithmetic and copies ran while one was open for 0% of the time, Pallas kernels for 0%

commit v1 on v0

--- a/solution.py
+++ b/solution.py
@@ -35,7 +35,10 @@
 
 def body(sketches, start_basis, shrink_index):
     size = lax.axis_size("rows")
-    strip = lax.all_to_all(sketches, "rows", split_axis=1, concat_axis=0, tiled=True)
+    count = lax.axis_size("rows")
+    blocks = jnp.stack(jnp.split(sketches, count, axis=1), axis=0)
+    blocks = lax.all_to_all(blocks, "rows", split_axis=0, concat_axis=0)
+    strip = jnp.concatenate(blocks, axis=0)
     width = start_basis.shape[0] // size
     own_basis = lax.dynamic_slice_in_dim(start_basis, lax.axis_index("rows") * width, width, 0)
     projected = all_sum(jnp.dot(strip, own_basis, preferred_element_type=jnp.float32))

time: 802 us -> 811 us (1.011)
  no operation moved by 1% of the time
where the time goes in v1:
time: 811 us; the launch traced here: 806 us
  waiting for transfers between devices  448 us (55%)
  other arithmetic  175 us (22%)
  blocking collectives  76.4 us (9%)
  matrix products  48.1 us (6%)
  local copies, waits for them, and re-layouts  30.6 us (4%)
  between operations  18.9 us (2%)
    psum x3, waiting for transfers between devices, all_sum(): return lax.psum(values, AXES)  400 us
    another operation x20, other arithmetic, inverse_factor(): lower_factor = jnp.linalg.cholesky(gram_total)  103 us
    psum x1, blocking collectives, all_sum(): return lax.psum(values, AXES)  59.7 us
    another operation x7, other arithmetic, inverse_factor(): return jax.scipy.linalg.solve_triangular(lower_factor, identity, lower=True)  59.5 us
    all_to_all x1, waiting for transfers between devices, body(): blocks = lax.all_to_all(blocks, 'rows', split_axis=0, concat_axis=0)  48.3 us
    all_to_all x1, blocking collectives, body(): lax.all_to_all(scaled, 'rows', split_axis=0, concat_axis=1, tiled=True)  16.7 us
  transfers between devices with their start and end apart: 4, of which 4 were waited for; matrix products, arithmetic and copies ran while one was open for 0% of the time, Pallas kernels for 0%

profile of v1, /device:TPU:0, one launch (start us, length us, event | category | flops | bytes accessed | tf_op | source)
XLA Modules:
  0.0 805.6 jit_solution(9574993742333280356)
XLA Ops:
  6.5 1.8 bitcast_dynamic-update-slice_fusion.10
  8.4 1.7 bitcast_dynamic-update-slice_fusion.9
  10.0 1.7 bitcast_dynamic-update-slice_fusion.8
  11.7 1.7 bitcast_dynamic-update-slice_fusion.7
  13.4 1.7 bitcast_dynamic-update-slice_fusion.6
  15.1 1.7 bitcast_dynamic-update-slice_fusion.5
  16.8 1.7 bitcast_dynamic-update-slice_fusion.4
  18.4 1.7 bitcast_dynamic-update-slice_fusion.3
  20.1 7.3 all-to-all-start
  27.5 48.3 %all-to-all-done = bf16[8,256,512]{2,1,0:T(8,128)(2,1)} async-done(((bf16[8,256,512]{2,1,0:T(8,128)(2,1)}), bf16[8,256,512]{2,1,0:T(8,128)(2,1)}, u32[]{:S(2)}, u32[]{:S(2)}) %all-to-all-start) | async-done | bytes 2097184 | tf_op jit(solution)/shard_map/all_to_all | solution.py:40
  75.8 3.6 fusion.43
  79.4 59.7 %all-reduce.11 = bf16[2048,256]{1,0:T(8,128)(2,1)S(1)} all-reduce(f32[2048,256]{1,0:T(8,128)} %fusion.43), channel_id=1, replica_groups=mesh['rows'=8,'cols'=4] {'rows','cols'}, use_global_device_ids=true, to_apply=%region_0.0 | all-reduce | flops 524288 | bytes 3145728 | tf_op jit(solution)/shard_map/psum | solution.py:27
  139.1 2.4 reduce-precision_convert_fusion.5
  141.5 3.4 fusion.4
  144.9 1.7 fusion.2
  147.0 133.4 %all-reduce.6.cloned.1.call-done = f32[2048,256]{1,0:T(8,128)} async-done(((f32[2048,256]{1,0:T(8,128)}), f32[2048,256]{1,0:T(8,128)}) %all-reduce.6.cloned.1.call-update) | async-done | bytes 2097168 | tf_op jit(solution)/shard_map/psum | solution.py:27
  280.4 3.8 fusion.89
  284.2 1.1 copy.4
  285.3 1.0 fusion.40
  286.5 11.7 %cholesky.172 = f32[128,128]{1,0:T(8,128)S(1)} custom-call(f32[128,128]{1,0:T(8,128)S(1)} %cholesky.270), custom_call_target="Cholesky" | custom-call | tf_op jit(solution)/shard_map/jit(cholesky)/cholesky | solution.py:31
  298.3 9.8 %custom-call.15 = f32[1,128,128]{1,2,0:T(8,128)S(1)} custom-call(f32[1,128,128]{2,1,0:T(8,128)S(1)} %get-tuple-element.83), custom_call_target="InvertDiagBlocksLowerTriangular" | custom-call | tf_op jit(solution)/shard_map/jit(cholesky)/cholesky | solution.py:31
  308.5 11.7 %cholesky.189 = f32[128,128]{1,0:T(8,128)S(1)} custom-call(f32[128,128]{1,0:T(8,128)S(1)} %convolution_subtract_fusion.5), custom_call_target="Cholesky" | custom-call | tf_op jit(solution)/shard_map/jit(cholesky)/cholesky | solution.py:31
  320.3 0.7 compare_reduce_fusion.4
  322.3 4.5 while.6
  323.5 1.4 bitcast_dynamic-update-slice_fusion.14
  325.5 1.4 bitcast_dynamic-update-slice_fusion.14
  326.8 19.7 %custom-call.16 = f32[2,128,128]{1,2,0:T(8,128)S(1)} custom-call(f32[2,128,128]{2,1,0:T(8,128)S(1)} %get-tuple-element.30), custom_call_target="InvertDiagBlocksLowerTriangular" | custom-call | tf_op jit(solution)/shard_map/jit(_solve_triangular)/triangular_solve | solution.py:33
  347.4 3.4 convolution_convert_fusion.1
  350.8 2.4 reduce-precision_convert_fusion.3
  353.2 3.4 fusion.10
  356.7 1.7 fusion.1
  358.6 133.4 %all-reduce.8.cloned.1.call-done = f32[2048,256]{1,0:T(8,128)} async-done(((f32[2048,256]{1,0:T(8,128)}), f32[2048,256]{1,0:T(8,128)}) %all-reduce.8.cloned.1.call-update) | async-done | bytes 2097168 | tf_op jit(solution)/shard_map/psum | solution.py:27
  492.1 3.8 fusion.87
  495.9 1.1 copy.6
  496.9 1.0 fusion.38
  498.1 11.7 %cholesky.206 = f32[128,128]{1,0:T(8,128)S(1)} custom-call(f32[128,128]{1,0:T(8,128)S(1)} %cholesky.273), custom_call_target="Cholesky" | custom-call | tf_op jit(solution)/shard_map/jit(cholesky)/cholesky | solution.py:31
  509.9 9.8 %custom-call.17 = f32[1,128,128]{1,2,0:T(8,128)S(1)} custom-call(f32[1,128,128]{2,1,0:T(8,128)S(1)} %get-tuple-element.79), custom_call_target="InvertDiagBlocksLowerTriangular" | custom-call | tf_op jit(solution)/shard_map/jit(cholesky)/cholesky | solution.py:31
  520.2 11.7 %cholesky.223 = f32[128,128]{1,0:T(8,128)S(1)} custom-call(f32[128,128]{1,0:T(8,128)S(1)} %convolution_subtract_fusion.4), custom_call_target="Cholesky" | custom-call | tf_op jit(solution)/shard_map/jit(cholesky)/cholesky | solution.py:31
  534.6 3.9 while.7
  535.2 1.4 bitcast_dynamic-update-slice_fusion.15
  537.1 1.4 bitcast_dynamic-update-slice_fusion.15
  538.5 20.1 %custom-call.18 = f32[2,128,128]{1,2,0:T(8,128)S(1)} custom-call(f32[2,128,128]{2,1,0:T(8,128)S(1)} %get-tuple-element.31), custom_call_target="InvertDiagBlocksLowerTriangular" | custom-call | tf_op jit(solution)/shard_map/jit(_solve_triangular)/triangular_solve | solution.py:33
  559.5 3.4 convolution_convert_fusion
  562.9 3.2 reduce-precision_convert_fusion.1
  566.1 3.4 fusion.16
  569.5 1.7 fusion
  571.9 132.8 %all-reduce.10.cloned.1.call-done = f32[2048,256]{1,0:T(8,128)} async-done(((f32[2048,256]{1,0:T(8,128)}), f32[2048,256]{1,0:T(8,128)}) %all-reduce.10.cloned.1.call-update) | async-done | bytes 2097168 | tf_op jit(solution)/shard_map/psum | solution.py:27
  704.7 3.8 fusion.88
  708.5 1.1 copy.8
  709.6 1.0 fusion.36
  710.8 11.7 %cholesky.240 = f32[128,128]{1,0:T(8,128)S(1)} custom-call(f32[128,128]{1,0:T(8,128)S(1)} %cholesky.276), custom_call_target="Cholesky" | custom-call | tf_op jit(solution)/shard_map/jit(cholesky)/cholesky | solution.py:31
  722.6 9.9 %custom-call.19 = f32[1,128,128]{1,2,0:T(8,128)S(1)} custom-call(f32[1,128,128]{2,1,0:T(8,128)S(1)} %get-tuple-element.75), custom_call_target="InvertDiagBlocksLowerTriangular" | custom-call | tf_op jit(solution)/shard_map/jit(cholesky)/cholesky | solution.py:31
  733.0 11.7 %cholesky.257 = f32[128,128]{1,0:T(8,128)S(1)} custom-call(f32[128,128]{1,0:T(8,128)S(1)} %convolution_subtract_fusion.3), custom_call_target="Cholesky" | custom-call | tf_op jit(solution)/shard_map/jit(cholesky)/cholesky | solution.py:31
  744.7 0.7 compare_reduce_fusion
  747.4 3.9 while.8
  748.0 1.3 bitcast_dynamic-update-slice_fusion.16
  749.9 1.3 bitcast_dynamic-update-slice_fusion.16
  751.2 19.7 %custom-call.20 = f32[2,128,128]{1,2,0:T(8,128)S(1)} custom-call(f32[2,128,128]{2,1,0:T(8,128)S(1)} %get-tuple-element.32), custom_call_target="InvertDiagBlocksLowerTriangular" | custom-call | tf_op jit(solution)/shard_map/jit(_solve_triangular)/triangular_solve | solution.py:33
  771.8 3.4 fusion.3
  775.3 3.3 sort.15
  778.7 0.7 dynamic_slice.8
  780.0 0.7 maximum_sqrt_fusion
  781.4 16.7 %all_to_all.24 = f32[8,32,512]{2,1,0:T(8,128)S(1)} all-to-all(f32[8,32,512]{2,1,0:T(8,128)S(1)} %bitcast.151), channel_id=1, replica_groups=mesh['rows'=8,'cols'=4] {'rows'}, dimensions={0} | all-to-all | bytes 1048576 | tf_op jit(solution)/shard_map/all_to_all | solution.py:58
  798.1 0.8 copy.11
  (70 shorter events, 11.9 us)
Async XLA Ops:
  6.5 69.2 %copy-start = (bf16[4096,256]{1,0:T(8,128)(2,1)S(1)}, bf16[4096,256]{1,0:T(8,128)(2,1)}, u32[]{:S(2)}) copy-start(bf16[4096,256]{1,0:T(8,128)(2,1)} %param.7) | copy-start | bytes 6291460
  20.1 55.7 %all-to-all-start = ((bf16[8,256,512]{2,1,0:T(8,128)(2,1)}), bf16[8,256,512]{2,1,0:T(8,128)(2,1)}, u32[]{:S(2)}, u32[]{:S(2)}) async-start(bf16[8,256,512]{2,1,0:T(8,128)(2,1)} %bitcast_dynamic-update-slice_fusion.3), calls=%async_computation | async-start | bytes 4194304 | tf_op jit(solution)/shard_map/all_to_all | solution.py:40
  27.4 253.0 %all-reduce.6.cloned.1.call-start = ((), (), s32[]{:S(2)}) async-start(), calls=%async_computation.2 | async-start | bytes 4194304 | tf_op jit(solution)/shard_map/psum | solution.py:27
  146.7 345.4 %all-reduce.8.cloned.1.call-start = ((), (), s32[]{:S(2)}) async-start(), calls=%async_computation.3 | async-start | bytes 4194304 | tf_op jit(solution)/shard_map/psum | solution.py:27
  358.4 346.3 %all-reduce.10.cloned.1.call-start = ((), (), s32[]{:S(2)}) async-start(), calls=%async_computation.4 | async-start | bytes 4194304 | tf_op jit(solution)/shard_map/psum | solution.py:27
  747.3 33.4 %copy-start.1 = (f32[512,256]{0,1:T(8,128)S(1)}, f32[512,256]{0,1:T(8,128)}, u32[]{:S(2)}) copy-start(f32[512,256]{0,1:T(8,128)} %get-tuple-element.88) | copy-start | bytes 1572868
Sparse Core Ops, SparseCore 0:
  146.8 133.6 all-reduce.5
  358.5 133.5 all-reduce.7
  571.4 133.3 all-reduce.9
